TPU v7x, 128 devices: a whole 4x4x4 slice. The times are simulated.
128 devices in a mesh: ta: 8 (over z_hi, y), ha: 2 (over core), wa: 8 (over z_lo, x).
Axes of the slice: x: 4, y: 4, z: 4 (z_hi: 2, z_lo: 2; z = z_hi * 2 + z_lo), core: 2. Of those that a mesh axis runs over, the one named last changes fastest.
Arguments:
- queries: bfloat16 [32, 32, 64, 768], P('ta', 'ha', 'wa'), may hold values from -64 to 64
- keys: bfloat16 [32, 32, 64, 768], P('ta', 'ha', 'wa'), may hold values from -4 to 4
- values: bfloat16 [32, 32, 64, 768], P('ta', 'ha', 'wa'), may hold values from -6 to 6
- text_keys: bfloat16 [256, 768], P(('ta', 'ha', 'wa')), may hold values from -5 to 5
- text_values: bfloat16 [256, 768], P(('ta', 'ha', 'wa')), may hold values from -6 to 6
Outputs:
- attended: bfloat16 [32, 32, 64, 768], P('ta', 'ha', 'wa')
All inputs are finite; a program needn't handle non-finite values.
Results may differ from a plain program's by a relative error of at most 0.0037.
Values may be sent and summed in bfloat16 or wider, within the bound.
No kernel may reach another device: no remote copies, remote signals or barrier semaphores. Data moves between devices by JAX's collectives and lax.ppermute only.
A program may use at most 192 MiB of HBM per device.

v0:
```python
import jax
import jax.numpy as jnp
from jax import lax
from jax.sharding import PartitionSpec as P

HEADS = 6
TILE_T = 4
TILE_H = 8
TILE_W = 8


def extended(value, sides, width):
    for axis, dim in sides:
        size, length = (lax.axis_size(axis), value.shape[dim])
        up = [(i, (i + 1) % size) for i in range(size - 1)]
        down = [(j, i) for i, j in up]
        last = lax.slice_in_dim(value, length - width, length, axis=dim)
        first = lax.slice_in_dim(value, 0, width, axis=dim)
        before = lax.ppermute(last, axis, up)
        after = lax.ppermute(first, axis, down)
        value = jnp.concatenate([before, value, after], axis=dim)
    return value


def attend(query_tile, key_tile, value_tile, keep, text_keys, text_values):
    keys_all = jnp.concatenate([key_tile, text_keys], 0)
    vals_all = jnp.concatenate([value_tile, text_values], 0)
    scores = jnp.einsum(
        "qhd,khd->hqk", query_tile, keys_all, preferred_element_type=jnp.float32
    ) * query_tile.shape[2] ** (-0.5)
    allowed = jnp.concatenate([keep, jnp.ones((text_keys.shape[0],), jnp.float32) > 0.5])
    scores = jnp.where(allowed[None, None, :], scores, jnp.float32(-1e30))
    top = jnp.max(scores, -1, keepdims=True)
    weights = jnp.exp(scores - top)
    total = jnp.sum(weights, -1)
    rounded = weights.astype(jnp.bfloat16)
    summed = jnp.einsum("hqk,khd->qhd", rounded, vals_all, preferred_element_type=jnp.float32)
    return (summed / jnp.transpose(total)[:, :, None]).astype(jnp.bfloat16)


def inside_tiles(position, count, devices):
    place = position * count + jnp.arange(count + 2, dtype=jnp.int32) - 1
    return (place >= 0) & (place < count * devices)


def per_device(queries, keys, values, text_keys, text_values):
    width = queries.shape[3] // HEADS
    local_kv = jnp.stack((keys, values))
    heads_here = HEADS
    count_t = queries.shape[0] // TILE_T
    count_h = queries.shape[1] // TILE_H
    count_w = queries.shape[2] // TILE_W
    chans = queries.shape[3]
    shape7 = (count_t, TILE_T, count_h, TILE_H, count_w, TILE_W, chans)
    grid_q = queries.reshape(shape7)
    both = local_kv.reshape((2,) + shape7)
    padded = extended(both, (("ta", 1), ("ha", 3), ("wa", 5)), 1)
    keep_h = inside_tiles(lax.axis_index("ha"), count_h, lax.axis_size("ha"))
    text_pair = jnp.stack((text_keys, text_values))
    text_full = lax.all_gather(text_pair, ("ta", "ha", "wa"), axis=1, tiled=True)
    text_full = text_full.reshape(2, -1, heads_here, width)
    keep_t = inside_tiles(lax.axis_index("ta"), count_t, lax.axis_size("ta"))
    keep_w = inside_tiles(lax.axis_index("wa"), count_w, lax.axis_size("wa"))
    row_list = []
    for tile_b in range(count_h):
        window = padded[:, 0:3, :, tile_b : tile_b + 3, :, 0:3].reshape(2, -1, heads_here, width)
        mask = (
            keep_t[:, None, None, None, None, None]
            & keep_h[tile_b : tile_b + 3][None, None, :, None, None, None]
            & keep_w[None, None, None, None, :, None]
        )
        mask = jnp.broadcast_to(mask, (3, TILE_T, 3, TILE_H, 3, TILE_W)).reshape(-1)
        query_tile = grid_q[0, :, tile_b, :, 0].reshape(-1, heads_here, width)
        result = attend(query_tile, window[0], window[1], mask, text_full[0], text_full[1])
        col_list = [result.reshape(TILE_T, TILE_H, TILE_W, chans)]
        row_list.append(jnp.stack(col_list))
    plane_list = [jnp.stack(row_list)]
    tiles = jnp.stack(plane_list)
    tiles = jnp.transpose(tiles, (0, 3, 1, 4, 2, 5, 6))
    tiles = tiles.reshape(queries.shape)
    return tiles


def solution(mesh):
    placed = (
        P("ta", "ha", "wa", None),
        P("ta", "ha", "wa", None),
        P("ta", "ha", "wa", None),
        P(("ta", "ha", "wa"), None),
        P(("ta", "ha", "wa"), None),
    )
    return jax.shard_map(
        per_device, mesh=mesh, in_specs=placed, out_specs=P("ta", "ha", "wa", None), check_vma=False
    )
```

profile of v0, /device:TPU:0, one launch (start us, length us, event | category | flops | bytes accessed | tf_op | source)
XLA Modules:
  0.0 919.0 jit_solution(13567890914744605254)
XLA Ops:
  0.0 1.6 pad_maximum_fusion.11
  1.6 1.3 collective-permute-start.1
  2.9 4.6 collective-permute-start
  7.6 32.0 %collective-permute-done.1 = bf16[2,1,4,2,8,1,8,768]{7,6,5,4,3,2,1,0:T(8,128)(2,1)S(1)} collective-permute-done((bf16[2,1,4,2,8,1,8,768]{7,6,5,4,3,2,1,0:T(8,128)(2,1)S(1)}, bf16[2,1,4,2,8,1,8,768]{7,6,5,4,3,2,1,0:T(8,128)(2,1)S(1)}, u32[]{:S(2)}, u32[]{:S(2)}) %collective-permute-start.1) | collective-permute-done | bytes 1572896 | tf_op jit(solution)/shard_map/ppermute | solution.py:20
  39.6 1.2 collective-permute-done
  40.8 1.7 pad_maximum_fusion.10
  42.5 0.5 fusion.47
  43.0 0.0 copy-start.9
  43.0 0.0 copy-start.10
  43.0 1.6 collective-permute-start.2
  44.6 1.3 collective-permute-start.3
  45.9 2.7 collective-permute-done.2
  48.6 2.4 collective-permute-done.3
  51.0 0.0 copy-done
  51.0 0.0 copy-done.1
  51.0 4.6 pad_maximum_fusion.9
  55.6 0.0 copy-done.2
  55.6 1.3 collective-permute-start.5
  56.9 0.0 copy-done.3
  56.9 8.2 collective-permute-start.4
  65.1 0.0 copy-done.9
  65.1 0.0 copy-done.10
  65.2 0.1 fusion.49
  65.2 0.1 broadcast_and_fusion.3
  65.3 0.1 broadcast_and_fusion.1
  65.4 0.1 broadcast_in_dim.22
  65.5 0.2 reshape.126
  65.8 0.1 broadcast_in_dim.25
  65.9 0.2 reshape.128
  66.2 0.6 concatenate.35
  66.8 515.9 %all_gather.3 = bf16[2,256,768]{2,0,1:T(2,128)(2,1)S(1)} all-gather(bf16[2,2,768]{2,0,1:T(2,128)(2,1)S(1)} %copy.51), channel_id=1, replica_groups=mesh['ta'=8,'ha'=2,'wa'=8] {'ta','ha','wa'}, dimensions={1}, use_global_device_ids=true | all-gather | bytes 792576 | tf_op jit(solution)/shard_map/all_gather | solution.py:60
  582.6 2.2 fusion.48
  584.9 2.8 copy.52
  587.7 2.2 copy.71
  589.9 0.9 copy.56
  590.8 1.9 slice_bitcast_fusion.1
  592.7 2.2 reshape_squeeze.6
  595.0 1.2 reshape_squeeze.7
  596.2 0.0 collective-permute-done.5
  596.2 0.0 collective-permute-done.4
  596.2 18.5 %pad_maximum_fusion = bf16[2,3,4,4,8,3,8,768]{7,6,5,4,3,2,1,0:T(8,128)(2,1)} fusion(bf16[2,3,4,4,8,1,8,768]{7,6,5,4,3,2,1,0:T(8,128)(2,1)} %collective-permute-done.5, bf16[2,3,4,1,8,1,8,768]{7,6,5,4,3,2,1,0:T(8,128)(2,1)} %copy-done.3, bf16[2,1,4,2,8,1,8,768]{7,6,5,4,3,2,1,0:T(8,128)(2,1)S(1)} %collective-permute-done.1, ...), kind=kLoop, calls=%fused_computation.12 | loop fusion | flops 99090432 | bytes 56623104 | tf_op jit(solution)/shard_map/concatenate | solution.py:21
  614.7 28.4 %fusion.46 = (bf16[1,3,4,3,8,3,8,768]{7,6,5,4,3,2,1,0:T(8,128)(2,1)}, bf16[1,3,4,3,8,3,8,768]{7,6,5,4,3,2,1,0:T(8,128)(2,1)}, bf16[1,3,4,3,8,3,8,768]{7,6,5,4,3,...) fusion(bf16[2,3,4,4,8,3,8,768]{7,6,5,4,3,2,1,0:T(8,128)(2,1)} %pad_maximum_fusion), kind=kLoop, calls=%fused_computation.57 | loop fusion | bytes 84934656 | tf_op jit(solution)/shard_map/slice | solution.py:74
  643.2 22.2 %squeeze.20 = bf16[6912,6,128]{2,1,0:T(8,128)(2,1)} reshape(bf16[1,3,4,3,8,3,8,768]{7,6,5,4,3,2,1,0:T(8,128)(2,1)} %get-tuple-element.5) | data formatting | bytes 21233664 | tf_op jit(solution)/shard_map/squeeze | solution.py:74
  665.4 17.3 %copy.53 = bf16[6912,6,128]{0,2,1:T(8,128)(2,1)} copy(bf16[6912,6,128]{2,1,0:T(8,128)(2,1)} %squeeze.20) | data formatting | bytes 21233664 | tf_op jit(solution)/shard_map/squeeze | solution.py:74
  682.7 22.2 %squeeze.25 = bf16[6912,6,128]{2,1,0:T(8,128)(2,1)} reshape(bf16[1,3,4,3,8,3,8,768]{7,6,5,4,3,2,1,0:T(8,128)(2,1)} %get-tuple-element.6) | data formatting | bytes 21233664 | tf_op jit(solution)/shard_map/squeeze | solution.py:74
  705.0 11.6 %copy.62 = bf16[6912,6,128]{2,0,1:T(8,128)(2,1)} copy(bf16[6912,6,128]{2,1,0:T(8,128)(2,1)} %squeeze.25) | data formatting | bytes 21233664 | tf_op jit(solution)/shard_map/squeeze | solution.py:74
  716.6 22.2 %squeeze.24 = bf16[6912,6,128]{2,1,0:T(8,128)(2,1)} reshape(bf16[1,3,4,3,8,3,8,768]{7,6,5,4,3,2,1,0:T(8,128)(2,1)} %get-tuple-element.7) | data formatting | bytes 21233664 | tf_op jit(solution)/shard_map/squeeze | solution.py:74
  738.8 17.2 %copy.61 = bf16[6912,6,128]{0,2,1:T(8,128)(2,1)} copy(bf16[6912,6,128]{2,1,0:T(8,128)(2,1)} %squeeze.24) | data formatting | bytes 21233664 | tf_op jit(solution)/shard_map/squeeze | solution.py:74
  756.1 22.2 %squeeze.22 = bf16[6912,6,128]{2,1,0:T(8,128)(2,1)} reshape(bf16[1,3,4,3,8,3,8,768]{7,6,5,4,3,2,1,0:T(8,128)(2,1)} %get-tuple-element.8) | data formatting | bytes 21233664 | tf_op jit(solution)/shard_map/squeeze | solution.py:74
  778.3 11.8 %copy.55 = bf16[6912,6,128]{2,0,1:T(8,128)(2,1)} copy(bf16[6912,6,128]{2,1,0:T(8,128)(2,1)} %squeeze.22) | data formatting | bytes 21233664 | tf_op jit(solution)/shard_map/squeeze | solution.py:74
  790.1 0.0 copy-done.5
  790.1 22.6 %bitcast_reduce_fusion.1 = (f32[6,256]{1,0:T(8,128)S(1)}, f32[6,7168,256]{2,1,0:T(8,128)}) fusion(pred[7168]{0:T(1024)(128)(4,1)S(1)} %concatenate.32, bf16[256,6,128]{2,1,0:T(8,128)(2,1)S(1)} %copy-done.5, bf16[256,6,128]{2,0,1:T(8,128)(2,1)S(1)} %copy-done.6, bf16[6912,6,128]{2,0,1:T(8,128)(2,1)} %copy.55), kind=kOutput, calls=%fused_computation.4 | convolution fusion | flops 2873620992 | bytes 55456768 | tf_op jit(solution)/shard_map/qhd,khd->hqk/dot_general | solution.py:28
  812.8 19.5 %fusion.2 = f32[6,256]{1,0:T(8,128)S(1)} fusion(f32[6,7168,256]{2,1,0:T(8,128)} %get-tuple-element.24, f32[6,256]{1,0:T(8,128)S(1)} %get-tuple-element.23, pred[7168]{0:T(1024)(128)(4,1)S(1)} %concatenate.32), kind=kLoop, calls=%fused_computation.8 | loop fusion | flops 44038656 | bytes 44059648 | tf_op jit(solution)/shard_map/reduce_sum | solution.py:35
  832.3 0.0 copy-start.4
  832.3 20.9 %fusion.33 = bf16[256,6,128]{0,2,1:T(8,128)(2,1)S(1)} fusion(f32[6,7168,256]{2,1,0:T(8,128)} %get-tuple-element.24, f32[6,256]{1,0:T(8,128)S(1)} %get-tuple-element.23, pred[7168]{0:T(1024)(128)(4,1)S(1)} %concatenate.32, bf16[256,6,128]{0,2,1:T(8,128)(2,1)S(1)} %bitcast.92, bf16[6912,6,128]{0,2,1:T(8,128)(2,1)} %copy.53, f32[256,6]{0,1:T(8,128)S(1)} %bitcast.95), kind=kOutput, calls=%fused_computation.35 | convolution fusion | flops 2885025792 | bytes 55462912 | tf_op jit(solution)/shard_map/hqk,khd->qhd/dot_general | solution.py:37
  853.3 0.3 copy.60
  853.6 0.5 stack_stack_reshape.6
  854.1 22.7 %bitcast_reduce_fusion = (f32[6,256]{1,0:T(8,128)S(1)}, f32[6,7168,256]{2,1,0:T(8,128)}) fusion(pred[7168]{0:T(1024)(128)(4,1)S(1)} %copy-done.8, bf16[256,6,128]{2,1,0:T(8,128)(2,1)S(1)} %copy-done.4, bf16[256,6,128]{2,0,1:T(8,128)(2,1)S(1)} %copy-done.6, bf16[6912,6,128]{2,0,1:T(8,128)(2,1)} %copy.62), kind=kOutput, calls=%fused_computation.1 | convolution fusion | flops 2873620992 | bytes 55456768 | tf_op jit(solution)/shard_map/qhd,khd->hqk/dot_general | solution.py:28
  876.8 19.5 %fusion.4 = f32[6,256]{1,0:T(8,128)S(1)} fusion(f32[6,7168,256]{2,1,0:T(8,128)} %get-tuple-element.22, f32[6,256]{1,0:T(8,128)S(1)} %get-tuple-element.21, pred[7168]{0:T(1024)(128)(4,1)S(1)} %copy-done.8), kind=kLoop, calls=%fused_computation.10 | loop fusion | flops 44038656 | bytes 44059648 | tf_op jit(solution)/shard_map/reduce_sum | solution.py:35
  896.3 20.9 %fusion.27 = bf16[256,6,128]{0,2,1:T(8,128)(2,1)S(1)} fusion(f32[6,7168,256]{2,1,0:T(8,128)} %get-tuple-element.22, f32[6,256]{1,0:T(8,128)S(1)} %get-tuple-element.21, pred[7168]{0:T(1024)(128)(4,1)S(1)} %copy-done.8, bf16[256,6,128]{0,2,1:T(8,128)(2,1)S(1)} %bitcast.93, bf16[6912,6,128]{0,2,1:T(8,128)(2,1)} %copy.61, f32[256,6]{0,1:T(8,128)S(1)} %bitcast.94), kind=kOutput, calls=%fused_computation.33 | convolution fusion | flops 2885025792 | bytes 55462912 | tf_op jit(solution)/shard_map/hqk,khd->qhd/dot_general | solution.py:37
  917.2 0.3 copy.67
  917.5 0.5 stack_stack_reshape.7
  918.0 0.1 maximum_bitcast_fusion
  918.1 0.9 copy.68
  (17 shorter events, 0.1 us)
Async XLA Ops:
  0.0 51.0 %copy-start = (bf16[4,16,8,768]{3,2,1,0:T(8,128)(2,1)S(1)}, bf16[4,16,8,768]{3,2,1,0:T(8,128)(2,1)}, u32[]{:S(2)}) copy-start(bf16[4,16,8,768]{3,2,1,0:T(8,128)(2,1)} %param.7) | copy-start | bytes 2359300
  0.0 51.0 %copy-start.1 = (bf16[4,16,8,768]{3,2,1,0:T(8,128)(2,1)S(1)}, bf16[4,16,8,768]{3,2,1,0:T(8,128)(2,1)}, u32[]{:S(2)}) copy-start(bf16[4,16,8,768]{3,2,1,0:T(8,128)(2,1)} %param.6) | copy-start | bytes 2359300
  1.6 38.0 %collective-permute-start.1 = (bf16[2,1,4,2,8,1,8,768]{7,6,5,4,3,2,1,0:T(8,128)(2,1)S(1)}, bf16[2,1,4,2,8,1,8,768]{7,6,5,4,3,2,1,0:T(8,128)(2,1)S(1)}, u32[]{:S(2)}, u32[]{:S(2)}) collective-permute-start(bf16[2,1,4,2,8,1,8,768]{7,6,5,4,3,2,1,0:T(8,128)(2,1)S(1)} %pad_maximum_fusion.11), channel_id=1, source_target_pairs={{16,0},{32,16},{48,32},{64,48},{80,64},{96,80},{112,96},{17,1},{33... | collective-permute-start | bytes 4718600 | tf_op jit(solution)/shard_map/ppermute | solution.py:20
  2.9 37.8 %collective-permute-start = (bf16[2,1,4,2,8,1,8,768]{7,6,5,4,3,2,1,0:T(8,128)(2,1)S(1)}, bf16[2,1,4,2,8,1,8,768]{7,6,5,4,3,2,1,0:T(8,128)(2,1)S(1)}, u32[]{:S(2)}, u32[]{:S(2)}) collective-permute-start(bf16[2,1,4,2,8,1,8,768]{7,6,5,4,3,2,1,0:T(8,128)(2,1)S(1)} %pad_maximum_fusion.11), channel_id=1, source_target_pairs={{0,16},{16,32},{32,48},{48,64},{64,80},{80,96},{96,112},{1,17},{17... | collective-permute-start | bytes 4718600 | tf_op jit(solution)/shard_map/ppermute | solution.py:19
  43.0 22.1 %copy-start.9 = (bf16[2,768]{1,0:T(2,128)(2,1)S(1)}, bf16[2,768]{1,0:T(2,128)(2,1)}, u32[]{:S(2)}) copy-start(bf16[2,768]{1,0:T(2,128)(2,1)} %param.9) | copy-start | bytes 9220
  43.0 22.1 %copy-start.10 = (bf16[2,768]{1,0:T(2,128)(2,1)S(1)}, bf16[2,768]{1,0:T(2,128)(2,1)}, u32[]{:S(2)}) copy-start(bf16[2,768]{1,0:T(2,128)(2,1)} %param.8) | copy-start | bytes 9220
  43.0 5.6 collective-permute-start.2
  44.6 6.4 collective-permute-start.3
  48.6 7.0 copy-start.2
  51.0 5.8 copy-start.3
  55.6 540.6 %collective-permute-start.5 = (bf16[2,3,4,4,8,1,8,768]{7,6,5,4,3,2,1,0:T(8,128)(2,1)}, bf16[2,3,4,4,8,1,8,768]{7,6,5,4,3,2,1,0:T(8,128)(2,1)}, u32[]{:S(2)}, u32[]{:S(2)}) collective-permute-start(bf16[2,3,4,4,8,1,8,768]{7,6,5,4,3,2,1,0:T(8,128)(2,1)} %pad_maximum_fusion.9), channel_id=1, source_target_pairs={{1,0},{2,1},{3,2},{4,3},{5,4},{6,5},{7,6},{9,8},{10,9},{11,10},{12... | collective-permute-start | bytes 28311560 | tf_op jit(solution)/shard_map/ppermute | solution.py:20
  56.9 539.3 %collective-permute-start.4 = (bf16[2,3,4,4,8,1,8,768]{7,6,5,4,3,2,1,0:T(8,128)(2,1)}, bf16[2,3,4,4,8,1,8,768]{7,6,5,4,3,2,1,0:T(8,128)(2,1)}, u32[]{:S(2)}, u32[]{:S(2)}) collective-permute-start(bf16[2,3,4,4,8,1,8,768]{7,6,5,4,3,2,1,0:T(8,128)(2,1)} %pad_maximum_fusion.9), channel_id=1, source_target_pairs={{0,1},{1,2},{2,3},{3,4},{4,5},{5,6},{6,7},{8,9},{9,10},{10,11},{11... | collective-permute-start | bytes 28311560 | tf_op jit(solution)/shard_map/ppermute | solution.py:19
  778.3 11.8 %copy-start.5 = (bf16[256,6,128]{2,1,0:T(8,128)(2,1)S(1)}, bf16[256,6,128]{2,1,0:T(8,128)(2,1)}, u32[]{:S(2)}) copy-start(bf16[256,6,128]{2,1,0:T(8,128)(2,1)} %reshape_squeeze.6) | copy-start | bytes 1179652
  778.3 11.8 %copy-start.6 = (bf16[256,6,128]{2,0,1:T(8,128)(2,1)S(1)}, bf16[256,6,128]{2,0,1:T(8,128)(2,1)}, u32[]{:S(2)}) copy-start(bf16[256,6,128]{2,0,1:T(8,128)(2,1)} %copy.56) | copy-start | bytes 1179652
  812.8 19.5 %copy-start.7 = (bf16[1,256,768]{1,2,0:T(8,128)(2,1)S(1)}, bf16[1,256,768]{1,2,0:T(8,128)(2,1)}, u32[]{:S(2)}) copy-start(bf16[1,256,768]{1,2,0:T(8,128)(2,1)} %copy.52) | copy-start | bytes 1179652
  832.3 21.8 %copy-start.4 = (bf16[256,6,128]{2,1,0:T(8,128)(2,1)S(1)}, bf16[256,6,128]{2,1,0:T(8,128)(2,1)}, u32[]{:S(2)}) copy-start(bf16[256,6,128]{2,1,0:T(8,128)(2,1)} %reshape_squeeze.7) | copy-start | bytes 1179652
  832.3 21.8 %copy-start.8 = (pred[7168]{0:T(1024)(128)(4,1)S(1)}, pred[7168]{0:T(1024)(128)(4,1)}, u32[]{:S(2)}) copy-start(pred[7168]{0:T(1024)(128)(4,1)} %concatenate.35) | copy-start | bytes 21508
where the time goes:
time: 923 us; the launch traced here: 919 us
  blocking collectives  516 us (56%)
  local copies, waits for them, and re-layouts  193 us (21%)
  matrix products  87.1 us (9%)
  other arithmetic  65.7 us (7%)
  waiting for transfers between devices  38.3 us (4%)
  starting transfers between devices  18.3 us (2%)
    all_gather x1, blocking collectives, per_device(): lax.all_gather(text_pair, ('ta', 'ha', 'wa'), axis=1, tiled=True)  516 us
    squeeze x4, local copies, waits for them, and re-layouts, per_device(): window[1]  79.1 us
    squeeze x4, local copies, waits for them, and re-layouts, per_device(): window[0]  67.9 us
    dot_general x2, matrix products, attend(): jnp.einsum('qhd,khd->hqk', query_tile, keys_all, preferred_element_type=j...  45.3 us
    dot_general x2, matrix products, attend(): jnp.einsum('hqk,khd->qhd', rounded, vals_all, preferred_element_type=jnp....  41.8 us
    reduce_sum x2, other arithmetic, attend(): total = jnp.sum(weights, -1)  39 us
    ppermute x3, waiting for transfers between devices, extended(): after = lax.ppermute(first, axis, down)  34.4 us
    slice x1, local copies, waits for them, and re-layouts, per_device(): window[1]  28.4 us
  transfers between devices with their start and end apart: 6, of which 4 were waited for; matrix products, arithmetic and copies ran while one was open for 2% of the time, Pallas kernels for 0%

commit v1 on v0

--- a/solution.py
+++ b/solution.py
@@ -57,7 +57,12 @@
     padded = extended(both, (("ta", 1), ("ha", 3), ("wa", 5)), 1)
     keep_h = inside_tiles(lax.axis_index("ha"), count_h, lax.axis_size("ha"))
     text_pair = jnp.stack((text_keys, text_values))
-    text_full = lax.all_gather(text_pair, ("ta", "ha", "wa"), axis=1, tiled=True)
+    text_full = jnp.concatenate(
+        lax.all_to_all(
+            jnp.stack([text_pair] * lax.axis_size(("ta", "ha", "wa"))), ("ta", "ha", "wa"), 0, 0
+        ),
+        axis=1,
+    )
     text_full = text_full.reshape(2, -1, heads_here, width)
     keep_t = inside_tiles(lax.axis_index("ta"), count_t, lax.axis_size("ta"))
     keep_w = inside_tiles(lax.axis_index("wa"), count_w, lax.axis_size("wa"))

time: 923 us -> 625 us (0.68)
  blocking collectives: 516 us -> 0 us
  waiting for transfers between devices: 38.3 us -> 238 us
  starting transfers between devices: 18.3 us -> 34.6 us
    all_gather x1 -> x0, blocking collectives: 516 us -> none  [per_device(): lax.all_gather(text_pair, ('ta', 'ha', 'wa'), axis=1, tiled=True)]
    all_to_all x0 -> x1, waiting for transfers between devices: none -> 199 us  [per_device(): lax.all_to_all(jnp.stack([text_pair] * lax.axis_size(('ta', 'ha', 'wa')))...]
    all_to_all x0 -> x1, starting transfers between devices: none -> 16.3 us  [per_device(): lax.all_to_all(jnp.stack([text_pair] * lax.axis_size(('ta', 'ha', 'wa')))...]
  transfers between devices with their start and end apart: 6 -> 7, of which waited for: 4 -> 5; matrix products, arithmetic and copies ran while one was open for 2% -> 3% of each run, Pallas kernels for 0% -> 0%
where the time goes in v1:
time: 625 us; the launch traced here: 620 us
  waiting for transfers between devices  238 us (38%)
  local copies, waits for them, and re-layouts  195 us (31%)
  matrix products  86.9 us (14%)
  other arithmetic  65.6 us (10%)
  starting transfers between devices  34.6 us (6%)
    all_to_all x1, waiting for transfers between devices, per_device(): lax.all_to_all(jnp.stack([text_pair] * lax.axis_size(('ta', 'ha', 'wa')))...  199 us
    squeeze x4, local copies, waits for them, and re-layouts, per_device(): window[1]  79 us
    squeeze x4, local copies, waits for them, and re-layouts, per_device(): window[0]  67.8 us
    dot_general x2, matrix products, attend(): jnp.einsum('qhd,khd->hqk', query_tile, keys_all, preferred_element_type=j...  45.1 us
    dot_general x2, matrix products, attend(): jnp.einsum('hqk,khd->qhd', rounded, vals_all, preferred_element_type=jnp....  41.8 us
    reduce_sum x2, other arithmetic, attend(): total = jnp.sum(weights, -1)  39 us
    ppermute x3, waiting for transfers between devices, extended(): after = lax.ppermute(first, axis, down)  34.4 us
    slice x1, local copies, waits for them, and re-layouts, per_device(): window[1]  28.4 us
  transfers between devices with their start and end apart: 7, of which 5 were waited for; matrix products, arithmetic and copies ran while one was open for 3% of the time, Pallas kernels for 0%

profile of v1, /device:TPU:0, one launch (start us, length us, event | category | flops | bytes accessed | tf_op | source)
XLA Modules:
  0.0 620.0 jit_solution(335027535919874556)
XLA Ops:
  0.0 1.6 pad_maximum_fusion.11
  1.6 1.3 collective-permute-start.1
  2.9 4.6 collective-permute-start
  7.6 32.0 %collective-permute-done.1 = bf16[2,1,4,2,8,1,8,768]{7,6,5,4,3,2,1,0:T(8,128)(2,1)S(1)} collective-permute-done((bf16[2,1,4,2,8,1,8,768]{7,6,5,4,3,2,1,0:T(8,128)(2,1)S(1)}, bf16[2,1,4,2,8,1,8,768]{7,6,5,4,3,2,1,0:T(8,128)(2,1)S(1)}, u32[]{:S(2)}, u32[]{:S(2)}) %collective-permute-start.1) | collective-permute-done | bytes 1572896 | tf_op jit(solution)/shard_map/ppermute | solution.py:20
  39.6 1.2 collective-permute-done
  40.8 1.7 pad_maximum_fusion.10
  42.5 0.5 fusion.47
  43.0 0.0 copy-start.8
  43.0 0.0 copy-start.9
  43.0 1.6 collective-permute-start.2
  44.6 1.3 collective-permute-start.3
  45.9 2.7 collective-permute-done.2
  48.6 2.4 collective-permute-done.3
  51.0 0.0 copy-done.1
  51.0 4.5 pad_maximum_fusion.9
  55.5 1.3 collective-permute-start.5
  56.8 8.2 %collective-permute-start.4 = (bf16[2,3,4,4,8,1,8,768]{7,6,5,4,3,2,1,0:T(8,128)(2,1)}, bf16[2,3,4,4,8,1,8,768]{7,6,5,4,3,2,1,0:T(8,128)(2,1)}, u32[]{:S(2)}, u32[]{:S(2)}) collective-permute-start(bf16[2,3,4,4,8,1,8,768]{7,6,5,4,3,2,1,0:T(8,128)(2,1)} %pad_maximum_fusion.9), channel_id=1, source_target_pairs={{0,1},{1,2},{2,3},{3,4},{4,5},{5,6},{6,7},{8,9},{9,10},{10,11},{11... | collective-permute-start | bytes 28311560 | tf_op jit(solution)/shard_map/ppermute | solution.py:19
  65.0 0.0 copy-done.8
  65.0 1.3 stack.24
  66.3 16.3 %all-to-all-start = ((bf16[128,2,2,768]{3,2,1,0:T(2,128)(2,1)}), bf16[128,2,2,768]{3,2,1,0:T(2,128)(2,1)}, u32[]{:S(2)}, u32[]{:S(2)}) async-start(bf16[128,2,2,768]{3,2,1,0:T(2,128)(2,1)} %stack.24), calls=%async_computation | async-start | bytes 1572864 | tf_op jit(solution)/shard_map/all_to_all | solution.py:61
  82.7 0.1 fusion.49
  82.8 0.1 broadcast_and_fusion.3
  82.9 0.1 broadcast_and_fusion.1
  82.9 0.1 broadcast_in_dim.22
  83.1 0.2 reshape.131
  83.3 0.1 broadcast_in_dim.25
  83.5 0.2 reshape.133
  83.7 0.6 concatenate.35
  84.3 1.9 slice_bitcast_fusion.1
  86.3 2.2 reshape_squeeze.6
  88.5 1.3 reshape_squeeze.7
  89.8 199.2 %all-to-all-done = bf16[128,2,2,768]{3,2,1,0:T(2,128)(2,1)} async-done(((bf16[128,2,2,768]{3,2,1,0:T(2,128)(2,1)}), bf16[128,2,2,768]{3,2,1,0:T(2,128)(2,1)}, u32[]{:S(2)}, u32[]{:S(2)}) %all-to-all-start) | async-done | bytes 786464 | tf_op jit(solution)/shard_map/all_to_all | solution.py:61
  289.0 2.4 fusion.48
  291.4 2.0 squeeze.21
  293.5 2.0 copy.52
  295.5 1.1 squeeze.23
  296.5 1.1 copy.54
  297.6 0.0 collective-permute-done.5
  297.6 0.0 collective-permute-done.4
  297.7 18.4 %pad_maximum_fusion = bf16[2,3,4,4,8,3,8,768]{7,6,5,4,3,2,1,0:T(8,128)(2,1)} fusion(bf16[2,3,4,4,8,1,8,768]{7,6,5,4,3,2,1,0:T(8,128)(2,1)} %collective-permute-done.5, bf16[2,3,4,1,8,1,8,768]{7,6,5,4,3,2,1,0:T(8,128)(2,1)} %copy-done.3, bf16[2,1,4,2,8,1,8,768]{7,6,5,4,3,2,1,0:T(8,128)(2,1)S(1)} %collective-permute-done.1, ...), kind=kLoop, calls=%fused_computation.12 | loop fusion | flops 99090432 | bytes 56623104 | tf_op jit(solution)/shard_map/concatenate | solution.py:21
  316.1 28.4 %fusion.46 = (bf16[1,3,4,3,8,3,8,768]{7,6,5,4,3,2,1,0:T(8,128)(2,1)}, bf16[1,3,4,3,8,3,8,768]{7,6,5,4,3,2,1,0:T(8,128)(2,1)}, bf16[1,3,4,3,8,3,8,768]{7,6,5,4,3,...) fusion(bf16[2,3,4,4,8,3,8,768]{7,6,5,4,3,2,1,0:T(8,128)(2,1)} %pad_maximum_fusion), kind=kLoop, calls=%fused_computation.57 | loop fusion | bytes 84934656 | tf_op jit(solution)/shard_map/slice | solution.py:79
  344.5 22.2 %squeeze.20 = bf16[6912,6,128]{2,1,0:T(8,128)(2,1)} reshape(bf16[1,3,4,3,8,3,8,768]{7,6,5,4,3,2,1,0:T(8,128)(2,1)} %get-tuple-element.5) | data formatting | bytes 21233664 | tf_op jit(solution)/shard_map/squeeze | solution.py:79
  366.7 17.3 %copy.51 = bf16[6912,6,128]{0,2,1:T(8,128)(2,1)} copy(bf16[6912,6,128]{2,1,0:T(8,128)(2,1)} %squeeze.20) | data formatting | bytes 21233664 | tf_op jit(solution)/shard_map/squeeze | solution.py:79
  384.0 22.2 %squeeze.25 = bf16[6912,6,128]{2,1,0:T(8,128)(2,1)} reshape(bf16[1,3,4,3,8,3,8,768]{7,6,5,4,3,2,1,0:T(8,128)(2,1)} %get-tuple-element.6) | data formatting | bytes 21233664 | tf_op jit(solution)/shard_map/squeeze | solution.py:79
  406.2 11.6 %copy.61 = bf16[6912,6,128]{2,0,1:T(8,128)(2,1)} copy(bf16[6912,6,128]{2,1,0:T(8,128)(2,1)} %squeeze.25) | data formatting | bytes 21233664 | tf_op jit(solution)/shard_map/squeeze | solution.py:79
  417.9 22.2 %squeeze.24 = bf16[6912,6,128]{2,1,0:T(8,128)(2,1)} reshape(bf16[1,3,4,3,8,3,8,768]{7,6,5,4,3,2,1,0:T(8,128)(2,1)} %get-tuple-element.7) | data formatting | bytes 21233664 | tf_op jit(solution)/shard_map/squeeze | solution.py:79
  440.1 17.2 %copy.59 = bf16[6912,6,128]{0,2,1:T(8,128)(2,1)} copy(bf16[6912,6,128]{2,1,0:T(8,128)(2,1)} %squeeze.24) | data formatting | bytes 21233664 | tf_op jit(solution)/shard_map/squeeze | solution.py:79
  457.3 22.2 %squeeze.22 = bf16[6912,6,128]{2,1,0:T(8,128)(2,1)} reshape(bf16[1,3,4,3,8,3,8,768]{7,6,5,4,3,2,1,0:T(8,128)(2,1)} %get-tuple-element.8) | data formatting | bytes 21233664 | tf_op jit(solution)/shard_map/squeeze | solution.py:79
  479.6 11.7 %copy.53 = bf16[6912,6,128]{2,0,1:T(8,128)(2,1)} copy(bf16[6912,6,128]{2,1,0:T(8,128)(2,1)} %squeeze.22) | data formatting | bytes 21233664 | tf_op jit(solution)/shard_map/squeeze | solution.py:79
  491.3 0.0 copy-done.5
  491.3 22.4 %bitcast_reduce_fusion.1 = (f32[6,256]{1,0:T(8,128)S(1)}, f32[6,7168,256]{2,1,0:T(8,128)}) fusion(pred[7168]{0:T(1024)(128)(4,1)S(1)} %concatenate.32, bf16[256,6,128]{2,1,0:T(8,128)(2,1)S(1)} %copy-done.5, bf16[256,6,128]{2,0,1:T(8,128)(2,1)S(1)} %copy.54, bf16[6912,6,128]{2,0,1:T(8,128)(2,1)} %copy.53), kind=kOutput, calls=%fused_computation.4 | convolution fusion | flops 2873620992 | bytes 55456768 | tf_op jit(solution)/shard_map/qhd,khd->hqk/dot_general | solution.py:28
  513.7 19.5 %fusion.2 = f32[6,256]{1,0:T(8,128)S(1)} fusion(f32[6,7168,256]{2,1,0:T(8,128)} %get-tuple-element.24, f32[6,256]{1,0:T(8,128)S(1)} %get-tuple-element.23, pred[7168]{0:T(1024)(128)(4,1)S(1)} %concatenate.32), kind=kLoop, calls=%fused_computation.8 | loop fusion | flops 44038656 | bytes 44059648 | tf_op jit(solution)/shard_map/reduce_sum | solution.py:35
  533.3 0.0 copy-done.6
  533.3 0.0 copy-start.4
  533.3 20.9 %fusion.33 = bf16[256,6,128]{0,2,1:T(8,128)(2,1)S(1)} fusion(f32[6,7168,256]{2,1,0:T(8,128)} %get-tuple-element.24, f32[6,256]{1,0:T(8,128)S(1)} %get-tuple-element.23, pred[7168]{0:T(1024)(128)(4,1)S(1)} %concatenate.32, bf16[256,6,128]{0,2,1:T(8,128)(2,1)S(1)} %copy-done.6, bf16[6912,6,128]{0,2,1:T(8,128)(2,1)} %copy.51, f32[256,6]{0,1:T(8,128)S(1)} %bitcast.95), kind=kOutput, calls=%fused_computation.35 | convolution fusion | flops 2885025792 | bytes 55462912 | tf_op jit(solution)/shard_map/hqk,khd->qhd/dot_general | solution.py:37
  554.2 0.3 copy.58
  554.6 0.5 stack_stack_reshape.6
  555.1 22.7 %bitcast_reduce_fusion = (f32[6,256]{1,0:T(8,128)S(1)}, f32[6,7168,256]{2,1,0:T(8,128)}) fusion(pred[7168]{0:T(1024)(128)(4,1)S(1)} %copy-done.7, bf16[256,6,128]{2,1,0:T(8,128)(2,1)S(1)} %copy-done.4, bf16[256,6,128]{2,0,1:T(8,128)(2,1)S(1)} %copy.54, bf16[6912,6,128]{2,0,1:T(8,128)(2,1)} %copy.61), kind=kOutput, calls=%fused_computation.1 | convolution fusion | flops 2873620992 | bytes 55456768 | tf_op jit(solution)/shard_map/qhd,khd->hqk/dot_general | solution.py:28
  577.7 19.5 %fusion.4 = f32[6,256]{1,0:T(8,128)S(1)} fusion(f32[6,7168,256]{2,1,0:T(8,128)} %get-tuple-element.22, f32[6,256]{1,0:T(8,128)S(1)} %get-tuple-element.21, pred[7168]{0:T(1024)(128)(4,1)S(1)} %copy-done.7), kind=kLoop, calls=%fused_computation.10 | loop fusion | flops 44038656 | bytes 44059648 | tf_op jit(solution)/shard_map/reduce_sum | solution.py:35
  597.2 20.9 %fusion.27 = bf16[256,6,128]{0,2,1:T(8,128)(2,1)S(1)} fusion(f32[6,7168,256]{2,1,0:T(8,128)} %get-tuple-element.22, f32[6,256]{1,0:T(8,128)S(1)} %get-tuple-element.21, pred[7168]{0:T(1024)(128)(4,1)S(1)} %copy-done.7, bf16[256,6,128]{0,2,1:T(8,128)(2,1)S(1)} %copy-done.6, bf16[6912,6,128]{0,2,1:T(8,128)(2,1)} %copy.59, f32[256,6]{0,1:T(8,128)S(1)} %bitcast.94), kind=kOutput, calls=%fused_computation.33 | convolution fusion | flops 2885025792 | bytes 55462912 | tf_op jit(solution)/shard_map/hqk,khd->qhd/dot_general | solution.py:37
  618.1 0.3 copy.66
  618.5 0.5 stack_stack_reshape.7
  618.9 0.1 maximum_bitcast_fusion
  619.0 0.9 copy.67
  (17 shorter events, 0.1 us)
Async XLA Ops:
  0.0 51.0 %copy-start = (bf16[4,16,8,768]{3,2,1,0:T(8,128)(2,1)S(1)}, bf16[4,16,8,768]{3,2,1,0:T(8,128)(2,1)}, u32[]{:S(2)}) copy-start(bf16[4,16,8,768]{3,2,1,0:T(8,128)(2,1)} %param.7) | copy-start | bytes 2359300
  0.0 51.0 %copy-start.1 = (bf16[4,16,8,768]{3,2,1,0:T(8,128)(2,1)S(1)}, bf16[4,16,8,768]{3,2,1,0:T(8,128)(2,1)}, u32[]{:S(2)}) copy-start(bf16[4,16,8,768]{3,2,1,0:T(8,128)(2,1)} %param.6) | copy-start | bytes 2359300
  1.6 38.0 %collective-permute-start.1 = (bf16[2,1,4,2,8,1,8,768]{7,6,5,4,3,2,1,0:T(8,128)(2,1)S(1)}, bf16[2,1,4,2,8,1,8,768]{7,6,5,4,3,2,1,0:T(8,128)(2,1)S(1)}, u32[]{:S(2)}, u32[]{:S(2)}) collective-permute-start(bf16[2,1,4,2,8,1,8,768]{7,6,5,4,3,2,1,0:T(8,128)(2,1)S(1)} %pad_maximum_fusion.11), channel_id=1, source_target_pairs={{16,0},{32,16},{48,32},{64,48},{80,64},{96,80},{112,96},{17,1},{33... | collective-permute-start | bytes 4718600 | tf_op jit(solution)/shard_map/ppermute | solution.py:20
  2.9 37.8 %collective-permute-start = (bf16[2,1,4,2,8,1,8,768]{7,6,5,4,3,2,1,0:T(8,128)(2,1)S(1)}, bf16[2,1,4,2,8,1,8,768]{7,6,5,4,3,2,1,0:T(8,128)(2,1)S(1)}, u32[]{:S(2)}, u32[]{:S(2)}) collective-permute-start(bf16[2,1,4,2,8,1,8,768]{7,6,5,4,3,2,1,0:T(8,128)(2,1)S(1)} %pad_maximum_fusion.11), channel_id=1, source_target_pairs={{0,16},{16,32},{32,48},{48,64},{64,80},{80,96},{96,112},{1,17},{17... | collective-permute-start | bytes 4718600 | tf_op jit(solution)/shard_map/ppermute | solution.py:19
  43.0 22.0 %copy-start.8 = (bf16[2,768]{1,0:T(2,128)(2,1)S(1)}, bf16[2,768]{1,0:T(2,128)(2,1)}, u32[]{:S(2)}) copy-start(bf16[2,768]{1,0:T(2,128)(2,1)} %param.9) | copy-start | bytes 9220
  43.0 22.0 %copy-start.9 = (bf16[2,768]{1,0:T(2,128)(2,1)S(1)}, bf16[2,768]{1,0:T(2,128)(2,1)}, u32[]{:S(2)}) copy-start(bf16[2,768]{1,0:T(2,128)(2,1)} %param.8) | copy-start | bytes 9220
  43.0 5.6 collective-permute-start.2
  44.6 6.4 %collective-permute-start.3 = (bf16[2,3,4,1,8,1,8,768]{7,6,5,4,3,2,1,0:T(8,128)(2,1)S(1)}, bf16[2,3,4,1,8,1,8,768]{7,6,5,4,3,2,1,0:T(8,128)(2,1)S(1)}, u32[]{:S(2)}, u32[]{:S(2)}) collective-permute-start(bf16[2,3,4,1,8,1,8,768]{7,6,5,4,3,2,1,0:T(8,128)(2,1)S(1)} %get-tuple-element.10), channel_id=1, source_target_pairs={{8,0},{9,1},{10,2},{11,3},{12,4},{13,5},{14,6},{15,7},{24,16},{25,... | collective-permute-start | bytes 7077896 | tf_op jit(solution)/shard_map/ppermute | solution.py:20
  48.6 6.9 %copy-start.2 = (bf16[2,3,4,1,8,1,8,768]{7,6,5,4,3,2,1,0:T(8,128)(2,1)}, bf16[2,3,4,1,8,1,8,768]{7,6,5,4,3,2,1,0:T(8,128)(2,1)S(1)}, u32[]{:S(2)}) copy-start(bf16[2,3,4,1,8,1,8,768]{7,6,5,4,3,2,1,0:T(8,128)(2,1)S(1)} %collective-permute-done.2) | copy-start | bytes 7077892
  51.0 5.8 copy-start.3
  55.5 242.1 %collective-permute-start.5 = (bf16[2,3,4,4,8,1,8,768]{7,6,5,4,3,2,1,0:T(8,128)(2,1)}, bf16[2,3,4,4,8,1,8,768]{7,6,5,4,3,2,1,0:T(8,128)(2,1)}, u32[]{:S(2)}, u32[]{:S(2)}) collective-permute-start(bf16[2,3,4,4,8,1,8,768]{7,6,5,4,3,2,1,0:T(8,128)(2,1)} %pad_maximum_fusion.9), channel_id=1, source_target_pairs={{1,0},{2,1},{3,2},{4,3},{5,4},{6,5},{7,6},{9,8},{10,9},{11,10},{12... | collective-permute-start | bytes 28311560 | tf_op jit(solution)/shard_map/ppermute | solution.py:20
  56.8 240.8 %collective-permute-start.4 = (bf16[2,3,4,4,8,1,8,768]{7,6,5,4,3,2,1,0:T(8,128)(2,1)}, bf16[2,3,4,4,8,1,8,768]{7,6,5,4,3,2,1,0:T(8,128)(2,1)}, u32[]{:S(2)}, u32[]{:S(2)}) collective-permute-start(bf16[2,3,4,4,8,1,8,768]{7,6,5,4,3,2,1,0:T(8,128)(2,1)} %pad_maximum_fusion.9), channel_id=1, source_target_pairs={{0,1},{1,2},{2,3},{3,4},{4,5},{5,6},{6,7},{8,9},{9,10},{10,11},{11... | collective-permute-start | bytes 28311560 | tf_op jit(solution)/shard_map/ppermute | solution.py:19
  66.3 222.6 %all-to-all-start = ((bf16[128,2,2,768]{3,2,1,0:T(2,128)(2,1)}), bf16[128,2,2,768]{3,2,1,0:T(2,128)(2,1)}, u32[]{:S(2)}, u32[]{:S(2)}) async-start(bf16[128,2,2,768]{3,2,1,0:T(2,128)(2,1)} %stack.24), calls=%async_computation | async-start | bytes 1572864 | tf_op jit(solution)/shard_map/all_to_all | solution.py:61
  479.6 11.7 %copy-start.5 = (bf16[256,6,128]{2,1,0:T(8,128)(2,1)S(1)}, bf16[256,6,128]{2,1,0:T(8,128)(2,1)}, u32[]{:S(2)}) copy-start(bf16[256,6,128]{2,1,0:T(8,128)(2,1)} %reshape_squeeze.6) | copy-start | bytes 1179652
  513.7 19.5 %copy-start.6 = (bf16[256,6,128]{0,2,1:T(8,128)(2,1)S(1)}, bf16[256,6,128]{0,2,1:T(8,128)(2,1)}, u32[]{:S(2)}) copy-start(bf16[256,6,128]{0,2,1:T(8,128)(2,1)} %copy.52) | copy-start | bytes 1179652
  533.3 21.8 %copy-start.4 = (bf16[256,6,128]{2,1,0:T(8,128)(2,1)S(1)}, bf16[256,6,128]{2,1,0:T(8,128)(2,1)}, u32[]{:S(2)}) copy-start(bf16[256,6,128]{2,1,0:T(8,128)(2,1)} %reshape_squeeze.7) | copy-start | bytes 1179652
  533.3 21.8 %copy-start.7 = (pred[7168]{0:T(1024)(128)(4,1)S(1)}, pred[7168]{0:T(1024)(128)(4,1)}, u32[]{:S(2)}) copy-start(pred[7168]{0:T(1024)(128)(4,1)} %concatenate.35) | copy-start | bytes 21508
